TPU v7x, 512 devices: a whole 4x8x8 slice. The times are simulated.
512 devices in a mesh: tp: 8 (over y), vocab: 64 (over x, z, core).
Axes of the slice: x: 4, y: 8, z: 8, core: 2. Of those that a mesh axis runs over, the one named last changes fastest.
Arguments:
- partials: float32 [8, 1024, 8192], P('tp', 'vocab'), may hold values from -2.5 to 2.5
- residual: bfloat16 [1024, 8192], P('vocab', 'tp'), may hold values from -16 to 16
- norm_gain: float32 [8192], P('tp'), may hold values from 0.5 to 1.5
- head_weight: bfloat16 [8192, 98304], P('tp', 'vocab'), may hold values from -8 to 8
- owners: int32 [1024], P('tp'), may hold values from 0 to 63, as said below
- allowed: int32 [1024, 256], P('tp'), may hold values from 0 to 768, as said below
- counts: int32 [1024], P('tp'), may hold values from 1 to 256, as said below
Outputs:
- allowed_logprobs: float32 [2048, 256, 128], P(('tp', 'vocab'))
Inputs may be any that keep to these rules, and one draw needn't show every extreme that they name: `owners`: within each group of 128 consecutive rows no owner has more than 4 rows, and one owner has exactly 4. `allowed`: block b holds vocabulary ids 128 * b to 128 * b + 127. The first counts[r] entries of a row are distinct and ascending, the rest equal 768; at most 4 of a row's blocks lie among blocks 12 * v to 12 * v + 11 for any v, and in each group of rows the rows of one owner reach 4 for every v. `counts`: each group of 128 consecutive rows has a row with 256.
All inputs are finite; a program needn't handle non-finite values.
Results may differ from a plain program's by a relative error of at most 0.00032.
Values sent between devices are 32-bit elements; how exact they have to be, the bound alone decides.
A program may use at most 64 MiB of HBM per device.

v0:
```python
import jax
import jax.numpy as jnp
from jax import lax
from jax.sharding import PartitionSpec as P

EPSILON = 1e-05
BLOCK = 128
KMAX = 4


def slot_ranks(owners):
    row_order = jnp.arange(owners.shape[0], dtype=jnp.int32)
    same_owner = (owners[:, None] == owners[None, :]) & (row_order[:, None] < row_order[None, :])
    return jnp.sum(same_owner.astype(jnp.int32), axis=0)


def tail(raw_logits, sumsq, width, owners, allowed, counts):
    vocab_count = lax.axis_size("vocab")
    vocab_index = lax.axis_index("vocab")
    own_rows, columns = raw_logits.shape
    blocks_here = columns // BLOCK
    list_width = allowed.shape[1]
    per_owner = 2 * own_rows // vocab_count
    positions = jnp.arange(list_width, dtype=jnp.int32)
    slot_rank = slot_ranks(owners)
    mine = jnp.where(positions[None, :] < counts[:, None], allowed, -1) - vocab_index * blocks_here
    here = jnp.arange(blocks_here, dtype=jnp.int32)
    present = jnp.any(mine[:, None, :] == here[None, :, None], axis=2).astype(jnp.int32)
    place = jnp.sum(jnp.where(here[:, None] < here[None, :], present[:, :, None], 0), axis=1)
    place = jnp.where(present > 0, place, -1)
    target_row = owners * per_owner + slot_rank
    slots = jnp.arange(vocab_count * per_owner, dtype=jnp.int32)
    to_slot = (target_row[None, :] == slots[:, None]).astype(jnp.float32)
    slot_index = jnp.arange(per_owner, dtype=jnp.int32)[:, None]
    owned_slot = ((owners[None, :] == vocab_index) & (slot_rank[None, :] == slot_index)).astype(
        jnp.int32
    )
    slot_lists = jnp.sum(owned_slot[:, :, None] * allowed[None, :, :], axis=1)
    slot_counts = jnp.sum(owned_slot * counts[None, :], axis=1)
    live_entry = positions[None, :] < slot_counts[:, None]
    source = jnp.clip(slot_lists // blocks_here, 0, vocab_count - 1)
    rank = jnp.zeros_like(source)
    for back in range(1, KMAX):
        earlier = jnp.pad(source, ((0, 0), (back, 0)), constant_values=-1)[:, :list_width]
        rank = rank + (earlier == source).astype(jnp.int32)
    table_row = (source * per_owner + slot_index) * (KMAX + 1) + jnp.minimum(rank, KMAX - 1)
    table_row = jnp.where(live_entry, table_row, 0)
    logits = raw_logits * lax.rsqrt(sumsq / width + EPSILON)[:, None]
    row_top = jnp.max(logits, axis=1)
    row_total = jnp.sum(jnp.exp(logits - row_top[:, None]), axis=1)
    picked = []
    for k in range(KMAX):
        chosen = jnp.zeros((own_rows, BLOCK), jnp.float32)
        for b in range(blocks_here):
            block = logits[:, b * BLOCK : (b + 1) * BLOCK]
            chosen = jnp.where((place[:, b] == k)[:, None], block, chosen)
        picked.append(chosen)
    lane = jnp.arange(BLOCK, dtype=jnp.int32)[None, :]
    picked.append(
        jnp.where(lane == 0, row_top[:, None], jnp.where(lane == 1, row_total[:, None], 0.0))
    )
    payload = jnp.concatenate(picked, axis=1)
    outgoing = jnp.dot(
        to_slot, payload, precision=lax.Precision.HIGHEST, preferred_element_type=jnp.float32
    ).reshape(vocab_count, per_owner, (KMAX + 1) * BLOCK)
    incoming = lax.all_to_all(outgoing, "vocab", split_axis=0, concat_axis=0, tiled=True)
    tops = incoming[:, :, KMAX * BLOCK]
    totals = incoming[:, :, KMAX * BLOCK + 1]
    big_top = jnp.max(tops, axis=0)
    big_total = jnp.sum(totals * jnp.exp(tops - big_top[None, :]), axis=0)
    shift = big_top + jnp.log(big_total)
    received = incoming.reshape(vocab_count * per_owner * (KMAX + 1), BLOCK)
    gathered = jnp.take(received, table_row, axis=0)
    return jnp.where(live_entry[:, :, None], gathered - shift[:, None, None], 0.0)


def body(partials, residual, norm_gain, head_weight, owners, allowed, counts):
    summed = lax.psum_scatter(partials, "tp", scatter_dimension=2, tiled=True)[0]
    hidden_rows = summed + residual.astype(jnp.float32)
    every_row = lax.all_gather(hidden_rows, "vocab", axis=0, tiled=True)
    square_part = jnp.sum(every_row * every_row, axis=1)
    scaled = (every_row * norm_gain).astype(jnp.bfloat16)
    head_terms = jnp.dot(scaled, head_weight, preferred_element_type=jnp.float32)
    raw_logits = lax.psum_scatter(head_terms, "tp", scatter_dimension=0, tiled=True)
    sumsq = lax.psum_scatter(square_part, "tp", scatter_dimension=0, tiled=True)
    width = head_weight.shape[0] * lax.axis_size("tp")
    return tail(raw_logits, sumsq, width, owners, allowed, counts)


def solution(mesh):
    placed = (
        P("tp", "vocab", None),
        P("vocab", "tp"),
        P("tp"),
        P("tp", "vocab"),
        P("tp"),
        P("tp", None),
        P("tp"),
    )
    return jax.shard_map(
        body, mesh=mesh, in_specs=placed, out_specs=P(("tp", "vocab"), None, None), check_vma=False
    )
```

profile of v0, /device:TPU:1, one launch (start us, length us, event | category | flops | bytes accessed | tf_op | source)
XLA Modules:
  0.0 280.3 jit_solution(17336991937507651582)
XLA Ops:
  6.5 0.0 copy-start
  6.5 0.0 reduce-scatter.3.cloned.1.call-start
  6.5 0.7 reduce-scatter.3.cloned.1.call-update
  7.3 0.0 all-gather.2.cloned.1.call-start
  7.3 43.3 %reduce-scatter.3.cloned.1.call-done = f32[1,16,1024]{2,1,0:T(8,128)} async-done(((f32[1,16,8192]{2,1,0:T(8,128)}), f32[1,16,1024]{2,1,0:T(8,128)}) %reduce-scatter.3.cloned.1.call-update) | async-done | bytes 65552 | tf_op jit(solution)/shard_map/reduce_scatter | solution.py:78
  50.6 1.5 bitcast_add_fusion
  52.1 0.0 all-gather.2.cloned.1.call-update
  52.1 0.0 reduce-scatter.5.cloned.1.call-start
  52.2 91.4 %all-gather.2.cloned.1.call-done = f32[1024,1024]{1,0:T(8,128)} async-done(((f32[16,1024]{1,0:T(8,128)}), f32[1024,1024]{1,0:T(8,128)}) %all-gather.2.cloned.1.call-update) | async-done | bytes 4194320 | tf_op jit(solution)/shard_map/all_gather | solution.py:80
  143.6 0.0 copy-done
  143.6 7.5 %fusion = f32[1024,1536]{1,0:T(8,128)} fusion(bf16[1024,1536]{1,0:T(8,128)(2,1)S(1)} %copy-done, f32[1024,1024]{1,0:T(8,128)} %all-gather.2.cloned.1.call-done, f32[1024]{0:T(1024)} %param.9), kind=kOutput, calls=%fused_computation.3 | convolution fusion | flops 3223322624 | bytes 13635584 | tf_op jit(solution)/shard_map/dot_general | solution.py:83
  151.2 0.0 copy-start.1
  151.2 0.0 copy-start.2
  151.2 0.0 copy-start.3
  151.2 0.0 reduce-scatter.5.cloned.1.call-update
  151.2 0.9 copy-done.1
  152.1 0.0 copy-done.2
  152.1 0.1 select_subtract_fusion
  152.2 0.3 fusion.2
  152.5 1.3 dynamic-slice
  154.4 0.0 copy-done.3
  154.4 0.1 convert_reduce_fusion
  154.5 0.1 select_reduce_fusion
  154.7 2.5 multiply_reduce_fusion
  157.3 14.9 %all-reduce.3 = f32[1024]{0:T(1024)S(1)} all-reduce(f32[1024]{0:T(1024)S(1)} %multiply_reduce_fusion), channel_id=4, replica_groups=mesh['tp'=8,'vocab'=64] {'tp'}, use_global_device_ids=true, to_apply=%region_8.9.clone | all-reduce | flops 1024 | bytes 8192
  172.1 0.1 fusion.17
  172.2 53.1 %reduce-scatter.5.cloned.1.call-done = f32[128,1536]{1,0:T(8,128)} async-done(((f32[1024,1536]{1,0:T(8,128)}), f32[128,1536]{1,0:T(8,128)}) %reduce-scatter.5.cloned.1.call-update) | async-done | bytes 786448 | tf_op jit(solution)/shard_map/reduce_scatter | solution.py:84
  225.3 1.3 fusion.18
  226.6 0.3 exponential_reduce_fusion
  226.9 0.3 select_dynamic-update-slice_fusion.4
  227.2 0.3 select_dynamic-update-slice_fusion.3
  227.4 0.3 select_dynamic-update-slice_fusion.2
  227.7 0.3 select_dynamic-update-slice_fusion.1
  228.0 0.1 select_dynamic-update-slice_fusion
  228.1 1.3 fusion.3
  229.4 2.1 reshape.93
  231.5 11.1 %all-to-all-start = ((f32[64,4,640]{2,1,0:T(4,128)}), f32[64,4,640]{2,1,0:T(4,128)}, u32[]{:S(2)}, u32[]{:S(2)}) async-start(f32[64,4,640]{2,1,0:T(4,128)} %reshape.93), calls=%async_computation.2 | async-start | bytes 1310720 | tf_op jit(solution)/shard_map/all_to_all | solution.py:66
  242.6 0.1 select_reduce_fusion.1
  242.8 0.2 multiply_reduce_fusion.1
  242.9 0.1 compare_and_fusion
  243.0 19.6 %all-to-all-done = f32[64,4,640]{2,1,0:T(4,128)} async-done(((f32[64,4,640]{2,1,0:T(4,128)}), f32[64,4,640]{2,1,0:T(4,128)}, u32[]{:S(2)}, u32[]{:S(2)}) %all-to-all-start) | async-done | bytes 655392 | tf_op jit(solution)/shard_map/all_to_all | solution.py:66
  262.7 1.2 fusion.19
  263.9 0.1 copy.17
  264.0 0.1 copy.18
  264.1 0.2 fusion.13
  264.3 2.2 reshape.94
  266.5 5.1 %gather_fusion = f32[1024,128]{1,0:T(8,128)} fusion(f32[1280,128]{1,0:T(8,128)} %reshape.94, s32[1024]{0:T(1024)S(1)} %broadcast_clamp_fusion), kind=kCustom, calls=%fused_computation | custom fusion | bytes 1052672 | tf_op jit(solution)/shard_map/jit(_take)/gather | solution.py:73
  271.6 2.2 subtract_select_fusion
  (14 shorter events, 0.1 us)
Async XLA Ops:
  6.5 137.1 %copy-start = (bf16[1024,1536]{1,0:T(8,128)(2,1)S(1)}, bf16[1024,1536]{1,0:T(8,128)(2,1)}, u32[]{:S(2)}) copy-start(bf16[1024,1536]{1,0:T(8,128)(2,1)} %param.10) | copy-start | bytes 9437188
  6.5 44.1 %reduce-scatter.3.cloned.1.call-start = ((), (), s32[]{:S(2)}) async-start(), calls=%async_computation.3 | async-start | bytes 589824 | tf_op jit(solution)/shard_map/reduce_scatter | solution.py:78
  7.3 136.4 %all-gather.2.cloned.1.call-start = ((), (), s32[]{:S(2)}) async-start(), calls=%async_computation.4 | async-start | bytes 4259840 | tf_op jit(solution)/shard_map/all_gather | solution.py:80
  52.1 173.1 %reduce-scatter.5.cloned.1.call-start = ((), (), s32[]{:S(2)}) async-start(), calls=%async_computation.5 | async-start | bytes 7077888 | tf_op jit(solution)/shard_map/reduce_scatter | solution.py:84
  151.2 0.9 copy-start.1
  151.2 0.9 copy-start.2
  151.2 3.2 %copy-start.3 = (s32[128]{0:T(128)S(1)}, s32[128]{0:T(128)}, u32[]{:S(2)}) copy-start(s32[128]{0:T(128)} %param.11) | copy-start | bytes 1540
  231.5 31.2 %all-to-all-start = ((f32[64,4,640]{2,1,0:T(4,128)}), f32[64,4,640]{2,1,0:T(4,128)}, u32[]{:S(2)}, u32[]{:S(2)}) async-start(f32[64,4,640]{2,1,0:T(4,128)} %reshape.93), calls=%async_computation.2 | async-start | bytes 1310720 | tf_op jit(solution)/shard_map/all_to_all | solution.py:66
Sparse Core Ops, SparseCore 0:
  10.1 40.4 reduce-scatter.2
  54.0 89.5 all-gather.1
  151.3 73.9 reduce-scatter.4
where the time goes:
time: 281 us; the launch traced here: 280 us
  waiting for transfers between devices  208 us (74%)
  blocking collectives  14.9 us (5%)
  between operations  14 us (5%)
  local copies, waits for them, and re-layouts  11.8 us (4%)
  other arithmetic  11.5 us (4%)
  starting transfers between devices  11.2 us (4%)
  matrix products  8.81 us (3%)
    all_gather x1, waiting for transfers between devices, body(): every_row = lax.all_gather(hidden_rows, 'vocab', axis=0, tiled=True)  91.4 us
    reduce_scatter x1, waiting for transfers between devices, body(): lax.psum_scatter(head_terms, 'tp', scatter_dimension=0, tiled=True)  53.1 us
    reduce_scatter x1, waiting for transfers between devices, body(): lax.psum_scatter(partials, 'tp', scatter_dimension=2, tiled=True)[0]  43.3 us
    all_to_all x1, waiting for transfers between devices, tail(): lax.all_to_all(outgoing, 'vocab', split_axis=0, concat_axis=0, tiled=True)  19.6 us
    unnamed x1, blocking collectives  14.9 us
    all_to_all x1, starting transfers between devices, tail(): lax.all_to_all(outgoing, 'vocab', split_axis=0, concat_axis=0, tiled=True)  11.1 us
    dot_general x1, matrix products, body(): jnp.dot(scaled, head_weight, preferred_element_type=jnp.float32)  7.54 us
  transfers between devices with their start and end apart: 4, of which 4 were waited for; matrix products, arithmetic and copies ran while one was open for 2% of the time, Pallas kernels for 0%

commit v1 on v0

--- a/solution.py
+++ b/solution.py
@@ -77,7 +77,9 @@
 def body(partials, residual, norm_gain, head_weight, owners, allowed, counts):
     summed = lax.psum_scatter(partials, "tp", scatter_dimension=2, tiled=True)[0]
     hidden_rows = summed + residual.astype(jnp.float32)
-    every_row = lax.all_gather(hidden_rows, "vocab", axis=0, tiled=True)
+    every_row = jnp.concatenate(
+        lax.all_to_all(jnp.stack([hidden_rows] * lax.axis_size("vocab")), "vocab", 0, 0), axis=0
+    )
     square_part = jnp.sum(every_row * every_row, axis=1)
     scaled = (every_row * norm_gain).astype(jnp.bfloat16)
     head_terms = jnp.dot(scaled, head_weight, preferred_element_type=jnp.float32)

time: 281 us -> 299 us (1.064)
  blocking collectives: 14.9 us -> 126 us
  waiting for transfers between devices: 208 us -> 115 us
    all_to_all x0 -> x1, blocking collectives: none -> 112 us  [body(): lax.all_to_all(jnp.stack([hidden_rows] * lax.axis_size('vocab')), 'vocab'...]
    all_gather x1 -> x0, waiting for transfers between devices: 91.4 us -> none  [body(): every_row = lax.all_gather(hidden_rows, 'vocab', axis=0, tiled=True)]
  transfers between devices with their start and end apart: 4 -> 3, of which waited for: 4 -> 3; matrix products, arithmetic and copies ran while one was open for 2% -> 2% of each run, Pallas kernels for 0% -> 0%
where the time goes in v1:
time: 299 us; the launch traced here: 298 us
  blocking collectives  126 us (42%)
  waiting for transfers between devices  115 us (38%)
  between operations  14.3 us (5%)
  local copies, waits for them, and re-layouts  13.8 us (5%)
  other arithmetic  11.5 us (4%)
  starting transfers between devices  11.1 us (4%)
  matrix products  6.58 us (2%)
    all_to_all x1, blocking collectives, body(): lax.all_to_all(jnp.stack([hidden_rows] * lax.axis_size('vocab')), 'vocab'...  112 us
    reduce_scatter x1, waiting for transfers between devices, body(): lax.psum_scatter(head_terms, 'tp', scatter_dimension=0, tiled=True)  51.8 us
    reduce_scatter x1, waiting for transfers between devices, body(): lax.psum_scatter(partials, 'tp', scatter_dimension=2, tiled=True)[0]  43.3 us
    all_to_all x1, waiting for transfers between devices, tail(): lax.all_to_all(outgoing, 'vocab', split_axis=0, concat_axis=0, tiled=True)  19.6 us
    unnamed x1, blocking collectives  13.6 us
    all_to_all x1, starting transfers between devices, tail(): lax.all_to_all(outgoing, 'vocab', split_axis=0, concat_axis=0, tiled=True)  11.1 us
  transfers between devices with their start and end apart: 3, of which 3 were waited for; matrix products, arithmetic and copies ran while one was open for 2% of the time, Pallas kernels for 0%

profile of v1, /device:TPU:1, one launch (start us, length us, event | category | flops | bytes accessed | tf_op | source)
XLA Modules:
  0.0 298.4 jit_solution(8261845734032989033)
XLA Ops:
  6.5 0.0 copy-start
  6.5 0.0 reduce-scatter.3.cloned.1.call-start
  6.5 0.7 reduce-scatter.3.cloned.1.call-update
  7.3 0.0 reduce-scatter.5.cloned.1.call-start
  7.3 43.3 %reduce-scatter.3.cloned.1.call-done = f32[1,16,1024]{2,1,0:T(8,128)} async-done(((f32[1,16,8192]{2,1,0:T(8,128)}), f32[1,16,1024]{2,1,0:T(8,128)}) %reduce-scatter.3.cloned.1.call-update) | async-done | bytes 65552 | tf_op jit(solution)/shard_map/reduce_scatter | solution.py:78
  50.6 0.8 bitcast_add_fusion
  51.5 0.5 stack.2
  52.0 0.0 copy-start.3
  52.0 112.0 %all_to_all.10 = f32[64,16,1024]{2,1,0:T(8,128)S(1)} all-to-all(f32[64,16,1024]{2,1,0:T(8,128)S(1)} %stack.2), channel_id=1, replica_groups=mesh['tp'=8,'vocab'=64] {'vocab'}, dimensions={0} | all-to-all | bytes 8388608 | tf_op jit(solution)/shard_map/all_to_all | solution.py:81
  164.0 0.0 copy-done.3
  164.0 0.0 copy-start.1
  164.0 0.6 fusion
  164.6 1.4 copy-done.1
  166.1 0.0 copy-done
  166.1 5.3 %fusion.19 = f32[1024,1536]{1,0:T(8,128)} fusion(bf16[1024,1024]{1,0:T(8,128)(2,1)S(1)} %fusion, bf16[1024,1536]{1,0:T(8,128)(2,1)S(1)} %copy-done), kind=kOutput, calls=%fused_computation.109 | convolution fusion | flops 3221225472 | bytes 11534336 | tf_op jit(solution)/shard_map/dot_general | solution.py:85
  171.4 0.0 copy-start.2
  171.4 0.0 copy-start.4
  171.4 0.0 copy-start.5
  171.4 0.0 reduce-scatter.5.cloned.1.call-update
  171.4 0.9 copy-done.2
  172.3 0.0 copy-done.4
  172.3 0.1 select_subtract_fusion
  172.4 0.3 fusion.1
  172.7 1.3 dynamic-slice
  174.6 0.0 copy-done.5
  174.7 0.1 convert_reduce_fusion
  174.8 0.1 select_reduce_fusion
  175.0 2.5 multiply_reduce_fusion
  177.5 0.1 reduce_sum.70
  177.6 13.6 %all-reduce.3 = f32[1024]{0:T(1024)S(1)} all-reduce(f32[1024]{0:T(1024)S(1)} %reduce_sum.70), channel_id=4, replica_groups=mesh['tp'=8,'vocab'=64] {'tp'}, use_global_device_ids=true, to_apply=%region_8.9.clone | all-reduce | flops 1024 | bytes 8192
  191.2 0.1 fusion.16
  191.3 51.8 %reduce-scatter.5.cloned.1.call-done = f32[128,1536]{1,0:T(8,128)} async-done(((f32[1024,1536]{1,0:T(8,128)}), f32[128,1536]{1,0:T(8,128)}) %reduce-scatter.5.cloned.1.call-update) | async-done | bytes 786448 | tf_op jit(solution)/shard_map/reduce_scatter | solution.py:86
  243.1 1.3 fusion.17
  244.4 0.3 exponential_reduce_fusion
  244.7 0.3 select_dynamic-update-slice_fusion.4
  245.0 0.3 select_dynamic-update-slice_fusion.3
  245.2 0.3 select_dynamic-update-slice_fusion.2
  245.5 0.3 select_dynamic-update-slice_fusion.1
  245.8 0.1 select_dynamic-update-slice_fusion
  245.9 1.3 fusion.2
  247.2 2.1 reshape.100
  249.3 11.1 %all-to-all-start.1 = ((f32[64,4,640]{2,1,0:T(4,128)}), f32[64,4,640]{2,1,0:T(4,128)}, u32[]{:S(2)}, u32[]{:S(2)}) async-start(f32[64,4,640]{2,1,0:T(4,128)} %reshape.100), calls=%async_computation.3 | async-start | bytes 1310720 | tf_op jit(solution)/shard_map/all_to_all | solution.py:66
  260.4 0.1 select_reduce_fusion.1
  260.5 0.2 multiply_reduce_fusion.1
  260.7 0.1 compare_and_fusion
  260.8 19.6 %all-to-all-done.1 = f32[64,4,640]{2,1,0:T(4,128)} async-done(((f32[64,4,640]{2,1,0:T(4,128)}), f32[64,4,640]{2,1,0:T(4,128)}, u32[]{:S(2)}, u32[]{:S(2)}) %all-to-all-start.1) | async-done | bytes 655392 | tf_op jit(solution)/shard_map/all_to_all | solution.py:66
  280.4 1.2 fusion.18
  281.7 0.1 copy.17
  281.8 0.1 copy.18
  281.9 0.2 fusion.12
  282.1 2.2 reshape.101
  284.3 5.1 %gather_fusion = f32[1024,128]{1,0:T(8,128)} fusion(f32[1280,128]{1,0:T(8,128)} %reshape.101, s32[1024]{0:T(1024)S(1)} %broadcast_clamp_fusion), kind=kCustom, calls=%fused_computation | custom fusion | bytes 1052672 | tf_op jit(solution)/shard_map/jit(_take)/gather | solution.py:73
  289.4 2.2 subtract_select_fusion
  (14 shorter events, 0.1 us)
Async XLA Ops:
  6.5 159.5 %copy-start = (bf16[1024,1536]{1,0:T(8,128)(2,1)S(1)}, bf16[1024,1536]{1,0:T(8,128)(2,1)}, u32[]{:S(2)}) copy-start(bf16[1024,1536]{1,0:T(8,128)(2,1)} %param.10) | copy-start | bytes 9437188
  6.5 44.1 %reduce-scatter.3.cloned.1.call-start = ((), (), s32[]{:S(2)}) async-start(), calls=%async_computation.4 | async-start | bytes 589824 | tf_op jit(solution)/shard_map/reduce_scatter | solution.py:78
  7.3 235.8 %reduce-scatter.5.cloned.1.call-start = ((), (), s32[]{:S(2)}) async-start(), calls=%async_computation.5 | async-start | bytes 7077888 | tf_op jit(solution)/shard_map/reduce_scatter | solution.py:86
  52.0 112.0 %copy-start.3 = (f32[1024]{0:T(1024)S(1)}, f32[1024]{0:T(1024)}, u32[]{:S(2)}) copy-start(f32[1024]{0:T(1024)} %param.9) | copy-start | bytes 12292
  164.0 2.0 copy-start.1
  171.4 0.9 copy-start.2
  171.4 0.9 copy-start.4
  171.4 3.2 %copy-start.5 = (s32[128]{0:T(128)S(1)}, s32[128]{0:T(128)}, u32[]{:S(2)}) copy-start(s32[128]{0:T(128)} %param.11) | copy-start | bytes 1540
  249.3 31.1 %all-to-all-start.1 = ((f32[64,4,640]{2,1,0:T(4,128)}), f32[64,4,640]{2,1,0:T(4,128)}, u32[]{:S(2)}, u32[]{:S(2)}) async-start(f32[64,4,640]{2,1,0:T(4,128)} %reshape.100), calls=%async_computation.3 | async-start | bytes 1310720 | tf_op jit(solution)/shard_map/all_to_all | solution.py:66
Sparse Core Ops, SparseCore 0:
  10.1 40.4 reduce-scatter.2
  171.5 71.4 reduce-scatter.4
